TPU v7x, 32 devices: a whole 2x2x4 slice. The times are simulated.
32 devices in a mesh: wide: 8 (over z, x), narrow: 4 (over y, core).
Axes of the slice: x: 2, y: 2, z: 4, core: 2. Of those that a mesh axis runs over, the one named last changes fastest.
Arguments:
- embeddings: bfloat16 [16384, 1024], P(('wide', 'narrow')), may hold values from -32 to 32
- valid: int32 [16384], P(('wide', 'narrow')), may hold values from 0 to 1, as said below
Outputs:
- whitened: bfloat16 [16384, 1024], P(('wide', 'narrow'))
Inputs may be any that keep to these rules, and one draw needn't show every extreme that they name: The first row of every aligned block of 16 rows has valid = 1.
All inputs are finite; a program needn't handle non-finite values.
Results may differ from a plain program's by a relative error of at most 0.001.
Values sent between devices are 32-bit elements; how exact they have to be, the bound alone decides.
No kernel may reach another device: no remote copies, remote signals or barrier semaphores. Data moves between devices by JAX's collectives and lax.ppermute only.
A program may use at most 64 MiB of HBM per device.

v0:
```python
import jax
import jax.numpy as jnp
from jax import lax
from jax.sharding import PartitionSpec as P


def shifted_scatter(gram, count_local, sums_local, center):
    return (
        gram
        - sums_local[:, None] * center[None, :]
        - center[:, None] * sums_local[None, :]
        + count_local * center[:, None] * center[None, :]
    )


def narrow_rows(term):
    return lax.psum_scatter(term, "narrow", scatter_dimension=0, tiled=True)


def on_device(embeddings, valid):
    width = embeddings.shape[1]
    narrow_count = lax.axis_size("narrow")
    row_span = width // narrow_count
    offset = lax.axis_index("narrow") * row_span
    mask_half = valid.astype(jnp.bfloat16)
    count_local = jnp.sum(valid.astype(jnp.float32))
    masked = embeddings * mask_half[:, None]
    gram = lax.dot_general(
        masked, embeddings, (((0,), (0,)), ((), ())), preferred_element_type=jnp.float32
    )
    sums_local = jnp.dot(mask_half[None, :], embeddings, preferred_element_type=jnp.float32)[0]
    count, sums = lax.psum((count_local, sums_local), ("wide", "narrow"))
    term = shifted_scatter(gram, count_local, sums_local, sums / count)
    level_rows = narrow_rows(term)
    own_rows = lax.psum(level_rows, "wide")
    center = sums / count
    cov_rows = own_rows / count
    ident_rows = (
        lax.broadcasted_iota(jnp.int32, (row_span, width), 0) + offset
        == lax.broadcasted_iota(jnp.int32, (row_span, width), 1)
    ).astype(jnp.float32)
    diag_block = lax.dynamic_slice_in_dim(cov_rows, offset, row_span, 1)
    trace_part = jnp.sum(jnp.diagonal(diag_block))
    square_part = jnp.sum(cov_rows * cov_rows)
    trace_cov, square_sum = lax.psum((trace_part, square_part), "narrow")
    ridge_add = 0.05 * trace_cov / width + 1e-06
    norm_frob = jnp.sqrt(square_sum + 2.0 * ridge_add * trace_cov + width * ridge_add * ridge_add)
    base_rows = (cov_rows + ridge_add * ident_rows) / norm_frob
    root_rows = (3.0 * ident_rows - base_rows) / 2.0
    root_full = lax.all_gather(root_rows, "narrow", axis=0, tiled=True)
    first = jnp.dot(
        base_rows, root_full, precision=lax.Precision.HIGHEST, preferred_element_type=jnp.float32
    )
    second = jnp.dot(
        first, root_full, precision=lax.Precision.HIGHEST, preferred_element_type=jnp.float32
    )
    factor = (3.0 * ident_rows - second) / 2.0
    root_rows = jnp.dot(
        factor, root_full, precision=lax.Precision.HIGHEST, preferred_element_type=jnp.float32
    )
    centered_x = embeddings.astype(jnp.float32) - center
    product = jnp.dot(
        centered_x,
        lax.all_gather(root_rows, "narrow", axis=0, tiled=True),
        precision=lax.Precision.HIGHEST,
        preferred_element_type=jnp.float32,
    )
    return (product / jnp.sqrt(norm_frob)).astype(jnp.bfloat16)


def solution(mesh):
    in_specs = (P(("wide", "narrow"), None), P(("wide", "narrow")))
    out_specs = P(("wide", "narrow"), None)
    return jax.shard_map(
        on_device, mesh=mesh, in_specs=in_specs, out_specs=out_specs, check_vma=False
    )
```

profile of v0, /device:TPU:0, one launch (start us, length us, event | category | flops | bytes accessed | tf_op | source)
XLA Modules:
  0.0 300.6 jit_solution(4755402428084836865)
XLA Ops:
  6.5 0.0 reduce-scatter.2.cloned.1.call-start
  6.5 0.7 convert_element_type.14
  7.2 1.3 convert_reduce_fusion
  8.5 1.5 fusion.11
  10.0 42.1 %all-reduce = (f32[1024]{0:T(1024)S(1)}, f32[]{:T(128)}) all-reduce(f32[1024]{0:T(1024)S(1)} %bitcast.12, f32[]{:T(128)} %convert_reduce_fusion), channel_id=1, replica_groups=mesh['wide'=8,'narrow'=4] {'wide','narrow'}, use_global_device_ids=true, to_apply=%region_0.0 | all-reduce | flops 1025 | bytes 8200 | tf_op jit(solution)/shard_map/psum | solution.py:32
  52.1 1.3 broadcast_multiply_fusion
  53.4 5.3 %multiply_add_fusion = f32[1024,1024]{1,0:T(8,128)} fusion(bf16[512,1024]{1,0:T(8,128)(2,1)} %param.2, f32[1024]{0:T(1024)S(1)} %get-tuple-element.11, f32[1024]{0:T(1024)S(1)} %bitcast.13, f32[1024]{0:T(1024)S(1)} %get-tuple-element.12, bf16[512]{0:T(512)(128)(2,1)S(1)} %convert_element_type.14), kind=kOutput, calls=%fused_computation.1 | convolution fusion | flops 1080557568 | bytes 5256192 | tf_op jit(solution)/shard_map/dot_general | solution.py:28
  58.7 0.0 reduce-scatter.2.cloned.1.call-update
  58.7 0.0 all-reduce.4.cloned.1.call-start
  58.8 44.7 %reduce-scatter.2.cloned.1.call-done = f32[256,1024]{1,0:T(8,128)} async-done(((f32[1024,1024]{1,0:T(8,128)}), f32[256,1024]{1,0:T(8,128)}) %reduce-scatter.2.cloned.1.call-update) | async-done | bytes 1048592 | tf_op jit(solution)/shard_map/reduce_scatter | solution.py:17
  103.5 0.0 all-reduce.4.cloned.1.call-update
  103.5 0.0 all-gather.3.cloned.1.call-start
  103.6 81.6 %all-reduce.4.cloned.1.call-done = f32[256,1024]{1,0:T(8,128)} async-done(((f32[256,1024]{1,0:T(8,128)}), f32[256,1024]{1,0:T(8,128)}) %all-reduce.4.cloned.1.call-update) | async-done | bytes 1048592 | tf_op jit(solution)/shard_map/psum | solution.py:35
  185.2 2.7 multiply_reduce_fusion
  188.0 2.3 gather_fusion
  190.4 0.7 reduce_sum.28
  191.0 7.2 %all-reduce.1 = (f32[]{:T(128)}, f32[]{:T(128)}) all-reduce(f32[]{:T(128)} %get-tuple-element.9, f32[]{:T(128)} %reduce_sum.28), channel_id=1, replica_groups=mesh['wide'=8,'narrow'=4] {'narrow'}, use_global_device_ids=true, to_apply=%region_8.9 | all-reduce | flops 2 | bytes 16 | tf_op jit(solution)/shard_map/psum | solution.py:45
  200.3 1.3 fusion.7
  201.6 0.0 all-gather.3.cloned.1.call-update
  201.6 0.2 all-gather.5.cloned.1.call-start
  201.8 33.4 %all-gather.3.cloned.1.call-done = f32[1024,1024]{1,0:T(8,128)} async-done(((f32[256,1024]{1,0:T(8,128)}), f32[1024,1024]{1,0:T(8,128)}) %all-gather.3.cloned.1.call-update) | async-done | bytes 4194320 | tf_op jit(solution)/shard_map/all_gather | solution.py:50
  235.2 0.0 copy-start
  235.2 6.1 %fusion.10 = f32[256,1024]{1,0:T(8,128)S(1)} fusion(f32[1024,1024]{1,0:T(8,128)} %all-gather.3.cloned.1.call-done, f32[256,1024]{1,0:T(8,128)S(1)} %get-tuple-element.10, f32[]{:T(128)S(6)} %sqrt.6, f32[]{:T(128)S(6)} %add.45, s32[256]{0:T(256)S(1)} %iota_add_fusion), kind=kOutput, calls=%fused_computation.23 | convolution fusion | flops 3222274048 | bytes 6292488 | tf_op jit(solution)/shard_map/dot_general | solution.py:51
  241.4 0.0 copy-done
  241.4 3.7 %fusion.4 = f32[256,1024]{1,0:T(8,128)S(1)} fusion(f32[256,1024]{1,0:T(8,128)S(1)} %fusion.10, f32[1024,1024]{1,0:T(8,128)S(1)} %copy-done, s32[256]{0:T(256)S(1)} %iota_add_fusion), kind=kOutput, calls=%fused_computation.9 | convolution fusion | flops 3222274048 | bytes 6292480 | tf_op jit(solution)/shard_map/dot_general | solution.py:54
  245.1 0.0 copy-start.1
  245.2 4.7 %fusion.12 = f32[256,1024]{1,0:T(8,128)} fusion(f32[256,1024]{1,0:T(8,128)S(1)} %fusion.4, f32[1024,1024]{1,0:T(8,128)S(1)} %copy-done), kind=kOutput, calls=%fused_computation.25 | convolution fusion | flops 3221225472 | bytes 6291456 | tf_op jit(solution)/shard_map/dot_general | solution.py:58
  249.8 0.0 all-gather.5.cloned.1.call-update
  249.9 34.6 %all-gather.5.cloned.1.call-done = f32[1024,1024]{1,0:T(8,128)} async-done(((f32[256,1024]{1,0:T(8,128)}), f32[1024,1024]{1,0:T(8,128)}) %all-gather.5.cloned.1.call-update) | async-done | bytes 4194320 | tf_op jit(solution)/shard_map/all_gather | solution.py:64
  284.5 0.0 copy-done.1
  284.5 9.6 %divide_convert_fusion = bf16[512,1024]{1,0:T(8,128)(2,1)} fusion(f32[1024,1024]{1,0:T(8,128)} %all-gather.5.cloned.1.call-done, bf16[512,1024]{1,0:T(8,128)(2,1)S(1)} %copy-done.1, f32[]{:T(128)S(6)} %sqrt.7, f32[1024]{0:T(1024)S(1)} %get-tuple-element.12), kind=kOutput, calls=%fused_computation.2 | convolution fusion | flops 6444548096 | bytes 6295556 | tf_op jit(solution)/shard_map/dot_general | solution.py:62
  (4 shorter events, 0.0 us)
Async XLA Ops:
  6.5 97.0 %reduce-scatter.2.cloned.1.call-start = ((), (), s32[]{:S(2)}) async-start(), calls=%async_computation.1 | async-start | bytes 5242880 | tf_op jit(solution)/shard_map/reduce_scatter | solution.py:17
  58.7 126.5 %all-reduce.4.cloned.1.call-start = ((), (), s32[]{:S(2)}) async-start(), calls=%async_computation.2 | async-start | bytes 2097152 | tf_op jit(solution)/shard_map/psum | solution.py:35
  103.5 131.7 %all-gather.3.cloned.1.call-start = ((), (), s32[]{:S(2)}) async-start(), calls=%async_computation.3 | async-start | bytes 5242880 | tf_op jit(solution)/shard_map/all_gather | solution.py:50
  201.6 82.9 %all-gather.5.cloned.1.call-start = ((), (), s32[]{:S(2)}) async-start(), calls=%async_computation.4 | async-start | bytes 5242880 | tf_op jit(solution)/shard_map/all_gather | solution.py:64
  235.2 6.1 %copy-start = (f32[1024,1024]{1,0:T(8,128)S(1)}, f32[1024,1024]{1,0:T(8,128)}, u32[]{:S(2)}) copy-start(f32[1024,1024]{1,0:T(8,128)} %all-gather.3.cloned.1.call-done) | copy-start | bytes 12582916
  245.1 39.3 %copy-start.1 = (bf16[512,1024]{1,0:T(8,128)(2,1)S(1)}, bf16[512,1024]{1,0:T(8,128)(2,1)}, u32[]{:S(2)}) copy-start(bf16[512,1024]{1,0:T(8,128)(2,1)} %param.2) | copy-start | bytes 3145732
Sparse Core Ops, SparseCore 0:
  58.9 44.6 reduce-scatter.1
  107.0 78.1 all-reduce.3
  201.7 33.4 all-gather.2
  250.0 34.4 all-gather.4
where the time goes:
time: 301 us
  waiting for transfers between devices  194 us (64%)
  blocking collectives  49.3 us (16%)
  matrix products  30.9 us (10%)
  between operations  15.3 us (5%)
  other arithmetic  7.97 us (3%)
    psum x1, waiting for transfers between devices, on_device(): own_rows = lax.psum(level_rows, 'wide')  81.6 us
    reduce_scatter x1, waiting for transfers between devices, narrow_rows(): return lax.psum_scatter(term, 'narrow', scatter_dimension=0, tiled=True)  44.7 us
    psum x1, blocking collectives, on_device(): count, sums = lax.psum((count_local, sums_local), ('wide', 'narrow'))  42.1 us
    all_gather x1, waiting for transfers between devices, on_device(): lax.all_gather(root_rows, 'narrow', axis=0, tiled=True)  34.6 us
    all_gather x1, waiting for transfers between devices, on_device(): root_full = lax.all_gather(root_rows, 'narrow', axis=0, tiled=True)  33.4 us
    dot_general x1, matrix products, on_device(): jnp.dot(centered_x, lax.all_gather(root_rows, 'narrow', axis=0, tiled=Tru...  9.62 us
    psum x1, blocking collectives, on_device(): trace_cov, square_sum = lax.psum((trace_part, square_part), 'narrow')  7.19 us
    dot_general x1, matrix products, on_device(): jnp.dot(base_rows, root_full, precision=lax.Precision.HIGHEST, preferred_...  6.13 us
  transfers between devices with their start and end apart: 4, of which 4 were waited for; matrix products, arithmetic and copies ran while one was open for 0% of the time, Pallas kernels for 0%

commit v1 on v0

--- a/solution.py
+++ b/solution.py
@@ -47,7 +47,14 @@
     norm_frob = jnp.sqrt(square_sum + 2.0 * ridge_add * trace_cov + width * ridge_add * ridge_add)
     base_rows = (cov_rows + ridge_add * ident_rows) / norm_frob
     root_rows = (3.0 * ident_rows - base_rows) / 2.0
-    root_full = lax.all_gather(root_rows, "narrow", axis=0, tiled=True)
+    ring = [root_rows]
+    for hop in range(3):
+        ring.append(lax.ppermute(ring[-1], "narrow", [(dev, (dev + 1) % 4) for dev in range(4)]))
+    root_full = jnp.roll(
+        jnp.concatenate(ring[::-1], axis=0),
+        (lax.axis_index("narrow") + 1) * ring[0].shape[0],
+        axis=0,
+    )
     first = jnp.dot(
         base_rows, root_full, precision=lax.Precision.HIGHEST, preferred_element_type=jnp.float32
     )

time: 301 us -> 310 us (1.030)
  waiting for transfers between devices: 194 us -> 203 us
    ppermute x0 -> x3, waiting for transfers between devices: none -> 42.8 us  [on_device(): lax.ppermute(ring[-1], 'narrow', [(dev, (dev + 1) % 4) for dev in range(4)])]
    all_gather x1 -> x0, waiting for transfers between devices: 33.4 us -> none  [on_device(): root_full = lax.all_gather(root_rows, 'narrow', axis=0, tiled=True)]
  transfers between devices with their start and end apart: 4 -> 6, of which waited for: 4 -> 6; matrix products, arithmetic and copies ran while one was open for 0% -> 0% of each run, Pallas kernels for 0% -> 0%
where the time goes in v1:
time: 310 us; the launch traced here: 309 us
  waiting for transfers between devices  203 us (65%)
  blocking collectives  49.3 us (16%)
  matrix products  28.6 us (9%)
  between operations  15.4 us (5%)
  other arithmetic  7.61 us (2%)
  local copies, waits for them, and re-layouts  5.24 us (2%)
    psum x1, waiting for transfers between devices, on_device(): own_rows = lax.psum(level_rows, 'wide')  81.7 us
    reduce_scatter x1, waiting for transfers between devices, narrow_rows(): return lax.psum_scatter(term, 'narrow', scatter_dimension=0, tiled=True)  44.7 us
    ppermute x3, waiting for transfers between devices, on_device(): lax.ppermute(ring[-1], 'narrow', [(dev, (dev + 1) % 4) for dev in range(4)])  42.8 us
    psum x1, blocking collectives, on_device(): count, sums = lax.psum((count_local, sums_local), ('wide', 'narrow'))  42.1 us
    all_gather x1, waiting for transfers between devices, on_device(): lax.all_gather(root_rows, 'narrow', axis=0, tiled=True)  33.6 us
    dot_general x1, matrix products, on_device(): jnp.dot(centered_x, lax.all_gather(root_rows, 'narrow', axis=0, tiled=Tru...  9.61 us
    psum x1, blocking collectives, on_device(): trace_cov, square_sum = lax.psum((trace_part, square_part), 'narrow')  7.19 us
  transfers between devices with their start and end apart: 6, of which 6 were waited for; matrix products, arithmetic and copies ran while one was open for 0% of the time, Pallas kernels for 0%

profile of v1, /device:TPU:0, one launch (start us, length us, event | category | flops | bytes accessed | tf_op | source)
XLA Modules:
  0.0 309.2 jit_solution(8714916684798740813)
XLA Ops:
  6.5 0.7 convert_element_type.14
  7.2 1.3 convert_reduce_fusion
  8.5 1.5 fusion.23
  10.0 42.1 %all-reduce = (f32[1024]{0:T(1024)S(1)}, f32[]{:T(128)}) all-reduce(f32[1024]{0:T(1024)S(1)} %bitcast.9, f32[]{:T(128)} %convert_reduce_fusion), channel_id=1, replica_groups=mesh['wide'=8,'narrow'=4] {'wide','narrow'}, use_global_device_ids=true, to_apply=%region_0.0 | all-reduce | flops 1025 | bytes 8200 | tf_op jit(solution)/shard_map/psum | solution.py:32
  52.1 1.3 broadcast_multiply_fusion
  53.4 5.3 %multiply_add_fusion = f32[1024,1024]{1,0:T(8,128)} fusion(bf16[512,1024]{1,0:T(8,128)(2,1)} %param.2, f32[1024]{0:T(1024)S(1)} %get-tuple-element.11, f32[1024]{0:T(1024)S(1)} %bitcast.10, f32[1024]{0:T(1024)S(1)} %get-tuple-element.12, bf16[512]{0:T(512)(128)(2,1)S(1)} %convert_element_type.14), kind=kOutput, calls=%fused_computation.1 | convolution fusion | flops 1080557568 | bytes 5256192 | tf_op jit(solution)/shard_map/dot_general | solution.py:28
  58.7 0.0 all-reduce.4.cloned.1.call-start
  58.8 44.7 %reduce-scatter.2.cloned.1.call-done = f32[256,1024]{1,0:T(8,128)} async-done(((f32[1024,1024]{1,0:T(8,128)}), f32[256,1024]{1,0:T(8,128)}) %reduce-scatter.2.cloned.1.call-update) | async-done | bytes 1048592 | tf_op jit(solution)/shard_map/reduce_scatter | solution.py:17
  103.5 0.0 all-gather.2.cloned.1.call-start
  103.6 81.7 %all-reduce.4.cloned.1.call-done = f32[256,1024]{1,0:T(8,128)} async-done(((f32[256,1024]{1,0:T(8,128)}), f32[256,1024]{1,0:T(8,128)}) %all-reduce.4.cloned.1.call-update) | async-done | bytes 1048592 | tf_op jit(solution)/shard_map/psum | solution.py:35
  185.3 2.7 multiply_reduce_fusion
  188.1 2.3 gather_fusion
  190.5 0.7 reduce_sum.28
  191.1 7.2 %all-reduce.1 = (f32[]{:T(128)}, f32[]{:T(128)}) all-reduce(f32[]{:T(128)} %get-tuple-element.9, f32[]{:T(128)} %reduce_sum.28), channel_id=1, replica_groups=mesh['wide'=8,'narrow'=4] {'narrow'}, use_global_device_ids=true, to_apply=%region_8.9 | all-reduce | flops 2 | bytes 16 | tf_op jit(solution)/shard_map/psum | solution.py:45
  200.4 0.3 fusion.17
  200.7 0.1 collective-permute-start
  200.8 14.2 %collective-permute-done = f32[256,1024]{1,0:T(8,128)S(1)} collective-permute-done((f32[256,1024]{1,0:T(8,128)S(1)}, f32[256,1024]{1,0:T(8,128)S(1)}, u32[]{:S(2)}, u32[]{:S(2)}) %collective-permute-start) | collective-permute-done | bytes 1048608 | tf_op jit(solution)/shard_map/ppermute | solution.py:52
  215.0 14.2 %collective-permute-done.1 = f32[256,1024]{1,0:T(8,128)S(1)} collective-permute-done((f32[256,1024]{1,0:T(8,128)S(1)}, f32[256,1024]{1,0:T(8,128)S(1)}, u32[]{:S(2)}, u32[]{:S(2)}) %collective-permute-start.1) | collective-permute-done | bytes 1048608 | tf_op jit(solution)/shard_map/ppermute | solution.py:52
  229.2 14.3 %collective-permute-done.2 = f32[256,1024]{1,0:T(8,128)} collective-permute-done((f32[256,1024]{1,0:T(8,128)S(1)}, f32[256,1024]{1,0:T(8,128)}, u32[]{:S(2)}, u32[]{:S(2)}) %collective-permute-start.2) | collective-permute-done | bytes 1048608 | tf_op jit(solution)/shard_map/ppermute | solution.py:52
  243.6 1.3 constant_dynamic-update-slice_fusion.7
  244.9 0.1 constant_dynamic-update-slice_fusion.6
  244.9 0.1 constant_dynamic-update-slice_fusion.5
  245.0 0.3 constant_dynamic-update-slice_fusion.4
  245.3 1.3 constant_dynamic-update-slice_fusion.3
  246.6 0.1 constant_dynamic-update-slice_fusion.2
  246.7 0.1 constant_dynamic-update-slice_fusion.1
  246.8 0.3 constant_dynamic-update-slice_fusion
  247.1 3.8 %fusion.4 = f32[256,1024]{1,0:T(8,128)S(1)} fusion(f32[2048,1024]{1,0:T(8,128)S(1)} %constant_dynamic-update-slice_fusion, s32[]{:T(128)S(6)} %select_n.22, f32[256,1024]{1,0:T(8,128)S(1)} %get-tuple-element.10, f32[]{:T(128)S(6)} %sqrt.6, f32[]{:T(128)S(6)} %add.58, s32[256]{0:T(256)S(1)} %iota_add_fusion), kind=kOutput, calls=%fused_computation.6 | convolution fusion | flops 3222274048 | bytes 6292492 | tf_op jit(solution)/shard_map/dot_general | solution.py:58
  250.9 3.7 %fusion.12 = f32[256,1024]{1,0:T(8,128)S(1)} fusion(f32[256,1024]{1,0:T(8,128)S(1)} %fusion.4, f32[2048,1024]{1,0:T(8,128)S(1)} %constant_dynamic-update-slice_fusion, s32[]{:T(128)S(6)} %select_n.22, s32[256]{0:T(256)S(1)} %iota_add_fusion), kind=kOutput, calls=%fused_computation.15 | convolution fusion | flops 3222274048 | bytes 6292484 | tf_op jit(solution)/shard_map/dot_general | solution.py:61
  254.7 4.7 %fusion = f32[256,1024]{1,0:T(8,128)} fusion(f32[256,1024]{1,0:T(8,128)S(1)} %fusion.12, f32[2048,1024]{1,0:T(8,128)S(1)} %constant_dynamic-update-slice_fusion, s32[]{:T(128)S(6)} %select_n.22), kind=kOutput, calls=%fused_computation.2 | convolution fusion | flops 3221225472 | bytes 6291460 | tf_op jit(solution)/shard_map/dot_general | solution.py:65
  259.4 33.6 %all-gather.2.cloned.1.call-done = f32[1024,1024]{1,0:T(8,128)} async-done(((f32[256,1024]{1,0:T(8,128)}), f32[1024,1024]{1,0:T(8,128)}) %all-gather.2.cloned.1.call-update) | async-done | bytes 4194320 | tf_op jit(solution)/shard_map/all_gather | solution.py:71
  293.0 9.6 %divide_convert_fusion = bf16[512,1024]{1,0:T(8,128)(2,1)} fusion(f32[1024,1024]{1,0:T(8,128)} %all-gather.2.cloned.1.call-done, bf16[512,1024]{1,0:T(8,128)(2,1)S(1)} %copy-done, f32[]{:T(128)S(6)} %sqrt.7, f32[1024]{0:T(1024)S(1)} %get-tuple-element.12), kind=kOutput, calls=%fused_computation.8 | convolution fusion | flops 6444548096 | bytes 6295556 | tf_op jit(solution)/shard_map/dot_general | solution.py:69
  (12 shorter events, 0.1 us)
Async XLA Ops:
  6.5 97.0 %reduce-scatter.2.cloned.1.call-start = ((), (), s32[]{:S(2)}) async-start(), calls=%async_computation.1 | async-start | bytes 5242880 | tf_op jit(solution)/shard_map/reduce_scatter | solution.py:17
  58.7 126.6 %all-reduce.4.cloned.1.call-start = ((), (), s32[]{:S(2)}) async-start(), calls=%async_computation.2 | async-start | bytes 2097152 | tf_op jit(solution)/shard_map/psum | solution.py:35
  103.5 189.5 %all-gather.2.cloned.1.call-start = ((), (), s32[]{:S(2)}) async-start(), calls=%async_computation.3 | async-start | bytes 5242880 | tf_op jit(solution)/shard_map/all_gather | solution.py:71
  200.7 14.3 %collective-permute-start = (f32[256,1024]{1,0:T(8,128)S(1)}, f32[256,1024]{1,0:T(8,128)S(1)}, u32[]{:S(2)}, u32[]{:S(2)}) collective-permute-start(f32[256,1024]{1,0:T(8,128)S(1)} %fusion.17), channel_id=1, source_target_pairs={{0,1},{1,2},{2,3},{3,0},{4,5},{5,6},{6,7},{7,4},{8,9},{9,10},{10,1... | collective-permute-start | bytes 3145736 | tf_op jit(solution)/shard_map/ppermute | solution.py:52
  215.0 14.2 %collective-permute-start.1 = (f32[256,1024]{1,0:T(8,128)S(1)}, f32[256,1024]{1,0:T(8,128)S(1)}, u32[]{:S(2)}, u32[]{:S(2)}) collective-permute-start(f32[256,1024]{1,0:T(8,128)S(1)} %collective-permute-done), channel_id=1, source_target_pairs={{0,1},{1,2},{2,3},{3,0},{4,5},{5,6},{6,7},{7,4},{8,9},{9,10},{10,1... | collective-permute-start | bytes 3145736 | tf_op jit(solution)/shard_map/ppermute | solution.py:52
  229.2 14.3 %collective-permute-start.2 = (f32[256,1024]{1,0:T(8,128)S(1)}, f32[256,1024]{1,0:T(8,128)}, u32[]{:S(2)}, u32[]{:S(2)}) collective-permute-start(f32[256,1024]{1,0:T(8,128)S(1)} %collective-permute-done.1), channel_id=1, source_target_pairs={{0,1},{1,2},{2,3},{3,0},{4,5},{5,6},{6,7},{7,4},{8,9},{9,10},{10,1... | collective-permute-start | bytes 3145736 | tf_op jit(solution)/shard_map/ppermute | solution.py:52
  250.9 42.1 %copy-start = (bf16[512,1024]{1,0:T(8,128)(2,1)S(1)}, bf16[512,1024]{1,0:T(8,128)(2,1)}, u32[]{:S(2)}) copy-start(bf16[512,1024]{1,0:T(8,128)(2,1)} %param.2) | copy-start | bytes 3145732
Sparse Core Ops, SparseCore 0:
  58.9 44.6 reduce-scatter.1
  107.0 78.2 all-reduce.3
  259.5 33.4 all-gather.1
